TPU v7x, 128 devices: a whole 4x4x4 slice. The times are simulated.
128 devices in a mesh: fsdp: 32 (over y, z, core), dp: 4 (over x).
Axes of the slice: x: 4, y: 4, z: 4, core: 2. Of those that a mesh axis runs over, the one named last changes fastest.
Arguments:
- tokens: bfloat16 [16384, 4096], P(('fsdp', 'dp')), may hold values from -6 to 6
- gain: float32 [4096], replicated, may hold values from 0.5 to 1.5
- tiles: bfloat16 [512, 128, 128], P('fsdp'), may hold values from -0.25 to 0.25
- tile_rows: int32 [512], replicated, may hold values from 0 to 31, as said below
- tile_cols: int32 [512], replicated, may hold values from 0 to 111, as said below
- cotangent: bfloat16 [16384, 14336], P(('fsdp', 'dp')), may hold values from -6 to 6
Outputs:
- projected: bfloat16 [16384, 14336], P(('fsdp', 'dp'))
- token_grad: bfloat16 [16384, 4096], P(('fsdp', 'dp'))
- tile_grad: float32 [512, 128, 128], P('fsdp')
- gain_grad: float32 [4096], replicated
Inputs may be any that keep to these rules, and one draw needn't show every extreme that they name: The pairs (tile_rows[i], tile_cols[i]) are all different. `tile_cols`: pairs with tile_rows as above.
All inputs are finite; a program needn't handle non-finite values.
Results may differ from a plain program's by a relative error of at most 0.0049.
Values may be sent and summed in bfloat16 or wider, within the bound.
No kernel may reach another device: no remote copies, remote signals or barrier semaphores. Data moves between devices by JAX's collectives and lax.ppermute only.
A program may use at most 256 MiB of HBM per device.

v0:
```python
import jax
import jax.numpy as jnp
from jax import lax
from jax.sharding import PartitionSpec as P


def shards(tokens, gain, tiles, tile_rows, tile_cols, cotangent):
    count = tokens.shape[0]
    width = tokens.shape[1]
    tile = tiles.shape[1]
    row_blocks = width // tile
    col_blocks = cotangent.shape[1] // tile
    x32 = tokens.astype(jnp.float32)
    scale = lax.rsqrt(jnp.mean(x32 * x32, axis=-1, keepdims=True) + 1e-05)
    normed = (x32 * scale * gain).astype(jnp.bfloat16)
    xblocks = normed.reshape(count, row_blocks, tile)
    gblocks = cotangent.reshape(count, col_blocks, tile)
    piece = lax.all_gather(tiles, "fsdp", axis=0, tiled=True)
    rows = tile_rows
    cols = tile_cols
    xsel = jnp.take(xblocks, rows, axis=1)
    gsel = jnp.take(gblocks, cols, axis=1)
    forward = jnp.einsum("tkj,kjm->tkm", xsel, piece, preferred_element_type=jnp.float32)
    backward = jnp.einsum("tkm,kjm->tkj", gsel, piece, preferred_element_type=jnp.float32)
    stacked = jnp.stack([forward, backward], axis=0)
    outsum = jnp.zeros((count, col_blocks, tile), jnp.float32).at[:, tile_cols].add(stacked[0])
    back = jnp.zeros((count, row_blocks, tile), jnp.float32).at[:, tile_rows].add(stacked[1])
    projected = outsum.reshape(count, col_blocks * tile).astype(jnp.bfloat16)
    dnormed = back.reshape(count, width)
    gain_grad = lax.psum(jnp.sum(dnormed * x32 * scale, axis=0), ("fsdp", "dp"))
    inner = jnp.mean(x32 * gain * dnormed, axis=-1, keepdims=True)
    token_grad = (scale * gain * dnormed - x32 * scale**3 * inner).astype(jnp.bfloat16)
    group = tiles.shape[0]
    number = tiles.shape[0] * lax.axis_size("fsdp")

    def group_terms(first):
        rows = lax.dynamic_slice_in_dim(tile_rows, first, group, 0)
        cols = lax.dynamic_slice_in_dim(tile_cols, first, group, 0)
        xsel = jnp.take(xblocks, rows, axis=1)
        gsel = jnp.take(gblocks, cols, axis=1)
        return jnp.einsum("tkj,tkm->kjm", xsel, gsel, preferred_element_type=jnp.float32)

    firsts = group * jnp.arange(number // group, dtype=jnp.int32)
    result = lax.map(group_terms, firsts)
    owned = lax.psum_scatter(
        result.reshape(number, tile, tile), "fsdp", scatter_dimension=0, tiled=True
    )
    tile_grad = lax.psum(owned, "dp")
    return (projected, token_grad, tile_grad, gain_grad)


def solution(mesh):
    placed = (
        P(("fsdp", "dp"), None),
        P(),
        P("fsdp", None, None),
        P(),
        P(),
        P(("fsdp", "dp"), None),
    )
    return jax.shard_map(
        shards,
        mesh=mesh,
        in_specs=placed,
        out_specs=(P(("fsdp", "dp"), None), P(("fsdp", "dp"), None), P("fsdp", None, None), P()),
        check_vma=False,
    )
```

profile of v0, /device:TPU:1, one launch (start us, length us, event | category | flops | bytes accessed | tf_op | source)
XLA Modules:
  0.0 814.4 jit_solution(1176212291491571832)
XLA Ops:
  8.0 6.1 copy.35
  14.0 6.0 copy.36
  21.7 16.2 %gather_fusion.3 = bf16[512,128,128]{2,1,0:T(8,128)(2,1)} fusion(bf16[128,112,128]{2,0,1:T(8,128)(2,1)} %copy.36, s32[1024]{0:T(1024)S(1)} %pad_clamp_fusion.2), kind=kCustom, calls=%fused_computation.3 | custom fusion | bytes 33556480 | tf_op jit(solution)/shard_map/jit(_take)/gather | solution.py:22
  38.5 48.0 %all-gather.2.cloned.1.call-done = bf16[512,128,128]{2,1,0:T(8,128)(2,1)} async-done(((bf16[16,128,128]{2,1,0:T(8,128)(2,1)}), bf16[512,128,128]{2,1,0:T(8,128)(2,1)}) %all-gather.2.cloned.1.call-update) | async-done | bytes 16777232 | tf_op jit(solution)/shard_map/all_gather | solution.py:18
  86.5 28.2 %fusion.9 = f32[512,128,128]{2,1,0:T(8,128)} fusion(bf16[512,128,128]{2,1,0:T(8,128)(2,1)} %all-gather.2.cloned.1.call-done, bf16[512,128,128]{2,1,0:T(8,128)(2,1)} %gather_fusion.3, pred[512]{0:T(512)(128)(4,1)S(1)} %compare_and_fusion.2), kind=kOutput, calls=%fused_computation.22 | convolution fusion | flops 2155872256 | bytes 67109376 | tf_op jit(solution)/shard_map/tkm,kjm->tkj/dot_general | solution.py:24
  115.0 66.1 %scatter_fusion.1 = f32[128,32,128]{2,0,1:T(8,128)S(1)} fusion(f32[128,32,128]{2,0,1:T(8,128)S(1)} %broadcast_in_dim.69, s32[512]{0:T(512)S(1)} %compare_select_fusion.2, f32[512,128,128]{2,1,0:T(8,128)} %fusion.9), kind=kCustom, calls=%fused_computation.5 | custom fusion | flops 8388608 | bytes 100665344 | tf_op jit(solution)/shard_map/scatter-add | solution.py:27
  185.5 2.8 fusion.24
  189.0 237.1 %while.10 = (s32[]{:T(128)}, f32[32,16,128,128]{3,2,1,0:T(8,128)}, s32[32]{0:T(128)S(1)}, s32[512]{0:T(512)S(1)}, bf16[128,32,128]{2,0,1:T(8,128)(2,1)S(1)}, /*i...) while((s32[]{:T(128)}, f32[32,16,128,128]{3,2,1,0:T(8,128)}, ...), condition=%wide.region_5.6_spmd, body=%wide.region_4.5_spmd.sunk | while | flops 67635392 | bytes 4203735 | solution.py:44
  199.0 2.7 gather_fusion
  213.9 2.7 gather_fusion
  228.7 2.7 gather_fusion
  250.9 2.7 gather_fusion
  317.6 2.7 gather_fusion
  325.0 2.7 gather_fusion
  347.2 2.7 gather_fusion
  426.4 15.0 %gather_fusion.2 = bf16[512,128,128]{2,1,0:T(8,128)(2,1)} fusion(bf16[128,32,128]{2,0,1:T(8,128)(2,1)S(1)} %get-tuple-element.182, s32[1024]{0:T(1024)S(1)} %pad_clamp_fusion.3), kind=kCustom, calls=%fused_computation.2 | custom fusion | bytes 33556480 | tf_op jit(solution)/shard_map/jit(_take)/gather | solution.py:21
  441.3 148.6 %reduce-scatter.2.cloned.1.call-done = f32[16,128,128]{2,1,0:T(8,128)} async-done(((f32[512,128,128]{2,1,0:T(8,128)}), f32[16,128,128]{2,1,0:T(8,128)}) %reduce-scatter.2.cloned.1.call-update) | async-done | bytes 1048592 | tf_op jit(solution)/shard_map/reduce_scatter | solution.py:45
  590.0 24.5 %fusion.11 = f32[512,128,128]{2,1,0:T(8,128)} fusion(bf16[512,128,128]{2,1,0:T(8,128)(2,1)} %all-gather.2.cloned.1.call-done, bf16[512,128,128]{2,1,0:T(8,128)(2,1)} %gather_fusion.2, pred[512]{0:T(512)(128)(4,1)S(1)} %compare_and_fusion.3), kind=kOutput, calls=%fused_computation.24 | convolution fusion | flops 2155872256 | bytes 67109376 | tf_op jit(solution)/shard_map/tkj,kjm->tkm/dot_general | solution.py:23
  614.5 3.8 broadcast_in_dim.64
  618.3 103.4 %scatter_fusion = f32[128,112,128]{2,0,1:T(8,128)} fusion(f32[128,112,128]{2,0,1:T(8,128)} %broadcast_in_dim.64, s32[512]{0:T(512)S(1)} %compare_select_fusion.3, f32[512,128,128]{2,1,0:T(8,128)} %fusion.11), kind=kCustom, calls=%fused_computation.4 | custom fusion | flops 8388608 | bytes 100665344 | tf_op jit(solution)/shard_map/scatter-add | solution.py:26
  721.7 5.8 convert_element_type.17
  727.5 6.1 copy.34
  733.6 6.1 copy.40
  741.0 64.6 %psum.15 = f32[4096]{0:T(1024)} all-reduce(f32[4096]{0:T(1024)S(1)} %get-tuple-element.68), channel_id=1, replica_groups=mesh['fsdp'=32,'dp'=4] {'fsdp','dp'}, use_global_device_ids=true, to_apply=%region_9.10 | all-reduce | flops 4096 | bytes 32768 | tf_op jit(solution)/shard_map/psum | solution.py:30
  (250 shorter events, 167.2 us)
Async XLA Ops:
  7.2 14.5 %copy-start.2 = (s32[512]{0:T(512)S(1)}, s32[512]{0:T(512)}, u32[]{:S(2)}) copy-start(s32[512]{0:T(512)} %param.12) | copy-start | bytes 6148
  7.2 79.4 %all-gather.2.cloned.1.call-start = ((), (), s32[]{:S(2)}) async-start(), calls=%async_computation.1 | async-start | bytes 17301504 | tf_op jit(solution)/shard_map/all_gather | solution.py:18
  7.9 582.1 %reduce-scatter.2.cloned.1.call-start = ((), (), s32[]{:S(2)}) async-start(), calls=%async_computation.2 | async-start | bytes 34603008 | tf_op jit(solution)/shard_map/reduce_scatter | solution.py:45
  21.7 16.8 %copy-start.3 = (s32[512]{0:T(512)S(1)}, s32[512]{0:T(512)}, u32[]{:S(2)}) copy-start(s32[512]{0:T(512)} %param.11) | copy-start | bytes 6148
  115.0 68.0 %copy-start.1 = (f32[4096]{0:T(1024)S(1)}, f32[4096]{0:T(1024)}, u32[]{:S(2)}) copy-start(f32[4096]{0:T(1024)} %param.9) | copy-start | bytes 49156
  426.1 379.5 %all-reduce.2.cloned.1.call-start = ((), (), s32[]{:S(2)}) async-start(), calls=%async_computation.3 | async-start | bytes 2097152 | tf_op jit(solution)/shard_map/psum | solution.py:48
  721.7 18.0 %copy-start = (bf16[128,4096]{0,1:T(8,128)(2,1)S(1)}, bf16[128,4096]{0,1:T(8,128)(2,1)}, u32[]{:S(2)}) copy-start(bf16[128,4096]{0,1:T(8,128)(2,1)} %get-tuple-element.90) | copy-start | bytes 3145732
Sparse Core Ops, SparseCore 0:
  10.3 76.2 all-gather.1
  426.2 163.6 reduce-scatter.1
  592.5 44.0 all-reduce.1
where the time goes:
time: 820 us; the launch traced here: 814 us
  waiting for transfers between devices  197 us (24%)
  local copies, waits for them, and re-layouts  192 us (23%)
  other arithmetic  184 us (22%)
  matrix products  98.3 us (12%)
  blocking collectives  64.6 us (8%)
  loops' own time  63.1 us (8%)
  between operations  13.9 us (2%)
    reduce_scatter x1, waiting for transfers between devices, shards(): lax.psum_scatter(result.reshape(number, tile, tile), 'fsdp', scatter_dime...  149 us
    scatter-add x1, other arithmetic, shards(): jnp.zeros((count, col_blocks, tile), jnp.float32).at[:, tile_cols]  103 us
    gather x32, local copies, waits for them, and re-layouts, group_terms(): gsel = jnp.take(gblocks, cols, axis=1)  85.9 us
    scatter-add x1, other arithmetic, shards(): jnp.zeros((count, row_blocks, tile), jnp.float32).at[:, tile_rows]  66.1 us
    psum x1, blocking collectives, shards(): gain_grad = lax.psum(jnp.sum(dnormed * x32 * scale, axis=0), ('fsdp', 'dp'))  64.6 us
    another operation x1, loops' own time, shards(): result = lax.map(group_terms, firsts)  63.1 us
    all_gather x1, waiting for transfers between devices, shards(): piece = lax.all_gather(tiles, 'fsdp', axis=0, tiled=True)  48 us
    dot_general x32, matrix products, group_terms(): jnp.einsum('tkj,tkm->kjm', xsel, gsel, preferred_element_type=jnp.float32)  45.6 us
  transfers between devices with their start and end apart: 3, of which 2 were waited for; matrix products, arithmetic and copies ran while one was open for 24% of the time, Pallas kernels for 0%

commit v1 on v0

--- a/solution.py
+++ b/solution.py
@@ -27,7 +27,7 @@
     back = jnp.zeros((count, row_blocks, tile), jnp.float32).at[:, tile_rows].add(stacked[1])
     projected = outsum.reshape(count, col_blocks * tile).astype(jnp.bfloat16)
     dnormed = back.reshape(count, width)
-    gain_grad = lax.psum(jnp.sum(dnormed * x32 * scale, axis=0), ("fsdp", "dp"))
+    gain_grad = lax.psum(lax.psum(jnp.sum(dnormed * x32 * scale, axis=0), "fsdp"), "dp")
     inner = jnp.mean(x32 * gain * dnormed, axis=-1, keepdims=True)
     token_grad = (scale * gain * dnormed - x32 * scale**3 * inner).astype(jnp.bfloat16)
     group = tiles.shape[0]

time: 820 us -> 898 us (1.095)
  blocking collectives: 64.6 us -> 135 us
    psum x1 -> x2, blocking collectives: 64.6 us -> 135 us  [the longest x1 121 us: shards(): lax.psum(jnp.sum(dnormed * x32 * scale, axis=0), 'fsdp')]
  transfers between devices with their start and end apart: 3 -> 3, of which waited for: 2 -> 2; matrix products, arithmetic and copies ran while one was open for 24% -> 22% of each run, Pallas kernels for 0% -> 0%
where the time goes in v1:
time: 898 us; the launch traced here: 885 us
  waiting for transfers between devices  197 us (22%)
  local copies, waits for them, and re-layouts  192 us (21%)
  other arithmetic  184 us (20%)
  blocking collectives  135 us (15%)
  matrix products  98.3 us (11%)
  loops' own time  63.1 us (7%)
  between operations  13.9 us (2%)
    reduce_scatter x1, waiting for transfers between devices, shards(): lax.psum_scatter(result.reshape(number, tile, tile), 'fsdp', scatter_dime...  149 us
    psum x1, blocking collectives, shards(): lax.psum(jnp.sum(dnormed * x32 * scale, axis=0), 'fsdp')  121 us
    scatter-add x1, other arithmetic, shards(): jnp.zeros((count, col_blocks, tile), jnp.float32).at[:, tile_cols]  103 us
    gather x32, local copies, waits for them, and re-layouts, group_terms(): gsel = jnp.take(gblocks, cols, axis=1)  85.9 us
    scatter-add x1, other arithmetic, shards(): jnp.zeros((count, row_blocks, tile), jnp.float32).at[:, tile_rows]  66.1 us
    another operation x1, loops' own time, shards(): result = lax.map(group_terms, firsts)  63.1 us
    all_gather x1, waiting for transfers between devices, shards(): piece = lax.all_gather(tiles, 'fsdp', axis=0, tiled=True)  48 us
    dot_general x32, matrix products, group_terms(): jnp.einsum('tkj,tkm->kjm', xsel, gsel, preferred_element_type=jnp.float32)  45.6 us
  transfers between devices with their start and end apart: 3, of which 2 were waited for; matrix products, arithmetic and copies ran while one was open for 22% of the time, Pallas kernels for 0%

profile of v1, /device:TPU:1, one launch (start us, length us, event | category | flops | bytes accessed | tf_op | source)
XLA Modules:
  0.0 885.0 jit_solution(12258507358059470691)
XLA Ops:
  8.0 6.1 copy.35
  14.0 6.0 copy.36
  21.7 16.2 %gather_fusion.3 = bf16[512,128,128]{2,1,0:T(8,128)(2,1)} fusion(bf16[128,112,128]{2,0,1:T(8,128)(2,1)} %copy.36, s32[1024]{0:T(1024)S(1)} %pad_clamp_fusion.2), kind=kCustom, calls=%fused_computation.3 | custom fusion | bytes 33556480 | tf_op jit(solution)/shard_map/jit(_take)/gather | solution.py:22
  38.5 48.0 %all-gather.2.cloned.1.call-done = bf16[512,128,128]{2,1,0:T(8,128)(2,1)} async-done(((bf16[16,128,128]{2,1,0:T(8,128)(2,1)}), bf16[512,128,128]{2,1,0:T(8,128)(2,1)}) %all-gather.2.cloned.1.call-update) | async-done | bytes 16777232 | tf_op jit(solution)/shard_map/all_gather | solution.py:18
  86.5 28.2 %fusion.9 = f32[512,128,128]{2,1,0:T(8,128)} fusion(bf16[512,128,128]{2,1,0:T(8,128)(2,1)} %all-gather.2.cloned.1.call-done, bf16[512,128,128]{2,1,0:T(8,128)(2,1)} %gather_fusion.3, pred[512]{0:T(512)(128)(4,1)S(1)} %compare_and_fusion.2), kind=kOutput, calls=%fused_computation.22 | convolution fusion | flops 2155872256 | bytes 67109376 | tf_op jit(solution)/shard_map/tkm,kjm->tkj/dot_general | solution.py:24
  115.0 66.1 %scatter_fusion.1 = f32[128,32,128]{2,0,1:T(8,128)S(1)} fusion(f32[128,32,128]{2,0,1:T(8,128)S(1)} %broadcast_in_dim.69, s32[512]{0:T(512)S(1)} %compare_select_fusion.2, f32[512,128,128]{2,1,0:T(8,128)} %fusion.9), kind=kCustom, calls=%fused_computation.5 | custom fusion | flops 8388608 | bytes 100665344 | tf_op jit(solution)/shard_map/scatter-add | solution.py:27
  185.5 2.8 fusion.24
  189.0 237.1 %while.10 = (s32[]{:T(128)}, f32[32,16,128,128]{3,2,1,0:T(8,128)}, s32[32]{0:T(128)S(1)}, s32[512]{0:T(512)S(1)}, bf16[128,32,128]{2,0,1:T(8,128)(2,1)S(1)}, /*i...) while((s32[]{:T(128)}, f32[32,16,128,128]{3,2,1,0:T(8,128)}, ...), condition=%wide.region_5.6_spmd, body=%wide.region_4.5_spmd.sunk | while | flops 67635392 | bytes 4203735 | solution.py:44
  199.0 2.7 gather_fusion
  213.9 2.7 gather_fusion
  228.7 2.7 gather_fusion
  250.9 2.7 gather_fusion
  317.6 2.7 gather_fusion
  325.0 2.7 gather_fusion
  426.4 15.0 %gather_fusion.2 = bf16[512,128,128]{2,1,0:T(8,128)(2,1)} fusion(bf16[128,32,128]{2,0,1:T(8,128)(2,1)S(1)} %get-tuple-element.182, s32[1024]{0:T(1024)S(1)} %pad_clamp_fusion.3), kind=kCustom, calls=%fused_computation.2 | custom fusion | bytes 33556480 | tf_op jit(solution)/shard_map/jit(_take)/gather | solution.py:21
  441.3 148.6 %reduce-scatter.2.cloned.1.call-done = f32[16,128,128]{2,1,0:T(8,128)} async-done(((f32[512,128,128]{2,1,0:T(8,128)}), f32[16,128,128]{2,1,0:T(8,128)}) %reduce-scatter.2.cloned.1.call-update) | async-done | bytes 1048592 | tf_op jit(solution)/shard_map/reduce_scatter | solution.py:45
  590.0 24.5 %fusion.11 = f32[512,128,128]{2,1,0:T(8,128)} fusion(bf16[512,128,128]{2,1,0:T(8,128)(2,1)} %all-gather.2.cloned.1.call-done, bf16[512,128,128]{2,1,0:T(8,128)(2,1)} %gather_fusion.2, pred[512]{0:T(512)(128)(4,1)S(1)} %compare_and_fusion.3), kind=kOutput, calls=%fused_computation.24 | convolution fusion | flops 2155872256 | bytes 67109376 | tf_op jit(solution)/shard_map/tkj,kjm->tkm/dot_general | solution.py:23
  614.5 3.8 broadcast_in_dim.64
  618.3 103.4 %scatter_fusion = f32[128,112,128]{2,0,1:T(8,128)} fusion(f32[128,112,128]{2,0,1:T(8,128)} %broadcast_in_dim.64, s32[512]{0:T(512)S(1)} %compare_select_fusion.3, f32[512,128,128]{2,1,0:T(8,128)} %fusion.11), kind=kCustom, calls=%fused_computation.4 | custom fusion | flops 8388608 | bytes 100665344 | tf_op jit(solution)/shard_map/scatter-add | solution.py:26
  721.7 5.8 convert_element_type.17
  727.5 6.1 copy.34
  733.6 6.1 copy.40
  741.0 121.3 %psum.22 = f32[4096]{0:T(1024)S(1)} all-reduce(f32[4096]{0:T(1024)S(1)} %get-tuple-element.68), channel_id=1, replica_groups=mesh['fsdp'=32,'dp'=4] {'fsdp'}, use_global_device_ids=true, to_apply=%region_9.10 | all-reduce | flops 4096 | bytes 32768 | tf_op jit(solution)/shard_map/psum | solution.py:30
  862.3 13.9 %psum.23 = f32[4096]{0:T(1024)} all-reduce(f32[4096]{0:T(1024)S(1)} %psum.22), channel_id=1, replica_groups=mesh['fsdp'=32,'dp'=4] {'dp'}, use_global_device_ids=true, to_apply=%region_10.11 | all-reduce | flops 4096 | bytes 32768 | tf_op jit(solution)/shard_map/psum | solution.py:30
  (251 shorter events, 169.9 us)
Async XLA Ops:
  7.2 14.5 %copy-start.2 = (s32[512]{0:T(512)S(1)}, s32[512]{0:T(512)}, u32[]{:S(2)}) copy-start(s32[512]{0:T(512)} %param.12) | copy-start | bytes 6148
  7.2 79.4 %all-gather.2.cloned.1.call-start = ((), (), s32[]{:S(2)}) async-start(), calls=%async_computation.1 | async-start | bytes 17301504 | tf_op jit(solution)/shard_map/all_gather | solution.py:18
  7.9 582.1 %reduce-scatter.2.cloned.1.call-start = ((), (), s32[]{:S(2)}) async-start(), calls=%async_computation.2 | async-start | bytes 34603008 | tf_op jit(solution)/shard_map/reduce_scatter | solution.py:45
  21.7 16.8 %copy-start.3 = (s32[512]{0:T(512)S(1)}, s32[512]{0:T(512)}, u32[]{:S(2)}) copy-start(s32[512]{0:T(512)} %param.11) | copy-start | bytes 6148
  115.0 68.0 %copy-start.1 = (f32[4096]{0:T(1024)S(1)}, f32[4096]{0:T(1024)}, u32[]{:S(2)}) copy-start(f32[4096]{0:T(1024)} %param.9) | copy-start | bytes 49156
  426.1 450.1 %all-reduce.2.cloned.1.call-start = ((), (), s32[]{:S(2)}) async-start(), calls=%async_computation.3 | async-start | bytes 2097152 | tf_op jit(solution)/shard_map/psum | solution.py:48
  721.7 18.0 %copy-start = (bf16[128,4096]{0,1:T(8,128)(2,1)S(1)}, bf16[128,4096]{0,1:T(8,128)(2,1)}, u32[]{:S(2)}) copy-start(bf16[128,4096]{0,1:T(8,128)(2,1)} %get-tuple-element.90) | copy-start | bytes 3145732
Sparse Core Ops, SparseCore 0:
  10.3 76.2 all-gather.1
  426.2 163.6 reduce-scatter.1
  592.5 44.0 all-reduce.1
